TPU v7x, 512 devices: a whole 4x8x8 slice. The times are simulated.
512 devices in a mesh: dp: 2 (over y_hi), gx: 32 (over x, z), gy: 8 (over y_lo, core).
Axes of the slice: x: 4, y: 8 (y_hi: 2, y_lo: 4; y = y_hi * 4 + y_lo), z: 8, core: 2. Of those that a mesh axis runs over, the one named last changes fastest.
Arguments:
- fields: bfloat16 [2, 16, 256, 32768], P('dp', None, 'gx', 'gy'), may hold values from -6 to 6
- pre_act: bfloat16 [2, 16, 256, 32768], P('dp', None, 'gx', 'gy'), may hold values from -6 to 6
- cotangent: bfloat16 [2, 16, 256, 32768], P('dp', None, 'gx', 'gy'), may hold values from -6 to 6
- spec_weight: bfloat16 [2, 32, 32, 16, 256], P(None, 'gx', None, 'gy'), may hold values from -12 to 12
- point_weight: bfloat16 [16, 16], replicated, may hold values from -1.5 to 1.5
Outputs:
- grad_fields: bfloat16 [2, 16, 256, 32768], P('dp', None, 'gx', 'gy')
- grad_spec: float32 [2, 32, 32, 16, 256], P(None, 'gx', None, 'gy')
All inputs are finite; a program needn't handle non-finite values.
Results may differ from a plain program's by a relative error of at most 0.0098.
Values may be sent and summed in bfloat16 or wider, within the bound.
No kernel may reach another device: no remote copies, remote signals or barrier semaphores. Data moves between devices by JAX's collectives and lax.ppermute only.
A program may use at most 64 MiB of HBM per device.

v0:
```python
import math

import jax
import jax.numpy as jnp
import numpy as np
from jax import lax
from jax.experimental import pallas as pl
from jax.experimental.pallas import tpu as pltpu
from jax.sharding import PartitionSpec as P

C = 16
NX = 256
NY = 512
NZ = 64
MX = 32
MY = 32
MZ = 16
GROUP = 8

F32 = jnp.float32
BF16 = jnp.bfloat16


def signed_freqs(kept, length):
    index = np.arange(kept)
    return np.where(index < kept // 2, index, length - kept + index)


def cos_sin(freqs, points, length):
    turns = points[:, None] * freqs[None, :] % length
    angle = turns.astype(np.float32) * np.float32(2.0 * math.pi / length)
    return np.cos(angle).astype(np.float32), np.sin(angle).astype(np.float32)


def z_block_table():
    cosine, sine = cos_sin(np.arange(MZ), np.arange(NZ), NZ)
    parts = np.stack([cosine.T, -sine.T], axis=1)
    same = np.eye(GROUP, dtype=np.float32)
    table = parts[:, :, None, None, :] * same[None, None, :, :, None]
    return table.reshape(2 * MZ * GROUP, GROUP * NZ).astype(BF16)


def y_block_tables(count, local_y, local_mz):
    cosine, sine = cos_sin(signed_freqs(MY, NY), np.arange(NY), NY)
    upper = np.stack([cosine, sine], axis=-1)
    lower = np.stack([-sine, cosine], axis=-1)
    table = np.stack([upper, lower], axis=0)
    table = table.reshape(2, count, local_y, MY, 2).transpose(1, 0, 3, 4, 2)
    same = np.eye(local_mz, dtype=np.float32)
    table = table[:, :, :, None, None, :, :] * same[None, None, None, :, :, None, None]
    return table.reshape(count, 2 * MY * local_mz, local_mz * 2 * local_y).astype(BF16)


def x_row_tables(count, local_x):
    cosine, sine = cos_sin(signed_freqs(MX, NX), np.arange(NX), NX)
    table = np.stack([cosine, sine], axis=0).reshape(2, count, local_x, MX)
    table = table.transpose(1, 0, 3, 2)
    return np.tile(table, (1, 1, 1, 128 // local_x)).astype(BF16)


def dot(left, right, dims):
    return lax.dot_general(left, right, (dims, ((), ())), preferred_element_type=F32)


def gelu_slope(value):
    cdf = 0.5 * (1.0 + lax.erf(value * (1.0 / math.sqrt(2.0))))
    return cdf + value * jnp.exp(-0.5 * value * value) * (1.0 / math.sqrt(2.0 * math.pi))


def copies_in(sources, targets, sems):
    width = targets[0].shape[1] // sems.shape[1]
    copies = []
    for chunk in range(sems.shape[1]):
        lanes = pl.ds(chunk * width, width)
        copies.append(
            [
                pltpu.make_async_copy(
                    source.at[:, lanes], target.at[:, lanes], sems.at[index, chunk]
                )
                for index, (source, target) in enumerate(zip(sources, targets))
            ]
        )
    return copies


def forward_zy(
    fields, pre_act, cotangent, z_source, y_source, grad_pre, kept, given,
    fields_in, pre_in, cotangent_in, z_table, y_table, lines, sems, table_sems,
):
    groups = pre_act.shape[1] // z_source.shape[1]
    per_chunk = groups // sems.shape[1]
    tables = [
        pltpu.make_async_copy(z_source, z_table, table_sems.at[0]),
        pltpu.make_async_copy(y_source.at[lax.axis_index("gy")], y_table, table_sems.at[1]),
    ]
    copies = copies_in(
        (pre_act, cotangent, fields), (pre_in, cotangent_in, fields_in), sems
    )
    for copy in copies[0] + tables[:1]:
        copy.start()
    for chunk in copies[1:]:
        for copy in chunk:
            copy.start()
    tables[1].start()
    width = pre_in.shape[1] // groups
    pair = []
    for group in range(groups):
        if group % per_chunk == 0:
            for copy in copies[group // per_chunk]:
                copy.wait()
        part = slice(group * width, (group + 1) * width)
        slope = gelu_slope(pre_in[:, part].astype(F32))
        grad = (cotangent_in[:, part].astype(F32) * slope).astype(BF16)
        grad_pre[:, part] = grad
        both = jnp.concatenate([fields_in[:, part], grad], axis=0)
        if group == 0:
            tables[0].wait()
        spectra = dot(z_table[...], both, ((1,), (1,)))
        pair.append(spectra.reshape(2 * MZ, GROUP, both.shape[0]))
        if len(pair) == 2:
            rows = slice((group - 1) * GROUP, (group + 1) * GROUP)
            lines[:, rows, :] = jnp.concatenate(pair, axis=1).astype(BF16)
            pair = []
    tables[1].wait()
    side = lax.axis_index("gy") % 2
    count = 2 * kept.shape[0]
    per = 2 * MZ // count
    for index in range(count // 2):
        for pieces, offset in ((given, 1 - side), (kept, side)):
            first = (2 * index + offset) * per
            block = lines[pl.ds(first, per)]
            block = block.reshape(per * block.shape[1], block.shape[2])
            pieces[index] = dot(y_table[...], block, ((1,), (0,))).astype(BF16)


def add_halves(kept, taken, sums):
    sums[...] = (kept[...].astype(F32) + taken[...].astype(F32)).astype(BF16)


def add_up(arrived):
    total = arrived[0].astype(F32)
    for index in range(1, arrived.shape[0]):
        total = total + arrived[index].astype(F32)
    return total


def x_blocks(x_rows):
    lanes = x_rows.shape[3]
    owner = lax.broadcasted_iota(jnp.int32, (C, lanes), 1) // (lanes // C)
    mask = owner == lax.broadcasted_iota(jnp.int32, (C, lanes), 0)
    rows = x_rows[lax.axis_index("gx")].astype(F32)
    blocks = []
    for part in range(2):
        table = jnp.where(mask[None], rows[part][:, None, :], 0.0)
        blocks.append(table.reshape(MX * C, lanes).astype(BF16))
    return blocks


def forward_x(arrived, x_rows, pieces):
    blocks = x_blocks(x_rows)
    total = add_up(arrived)
    half = total.shape[0] // 2
    swapped = jnp.concatenate([total[half:], -total[:half]], axis=0).astype(BF16)
    total = total.astype(BF16)
    lanes = blocks[0].shape[1]
    for part in range(2):
        own = slice(part * lanes, (part + 1) * lanes)
        spectra = dot(blocks[0], total[:, own], ((1,), (1,)))
        spectra = spectra + dot(blocks[1], swapped[:, own], ((1,), (1,)))
        spectra = spectra.reshape(MX, C, spectra.shape[1]).astype(BF16)
        pieces[:, part * C : (part + 1) * C, :] = spectra


def mode_scale(rows, local_mz):
    line = lax.broadcasted_iota(jnp.int32, (rows, 1), 0) % local_mz
    line = line + lax.axis_index("gy") * local_mz
    return jnp.where(line == 0, 1.0, 2.0).astype(F32) / float(NX * NY * NZ)


def repeat_tables():
    lane = lax.broadcasted_iota(jnp.int32, (C, C * C), 1)
    row = lax.broadcasted_iota(jnp.int32, (C, C * C), 0)
    outer = (lane // C == row).astype(F32)
    inner = (lane % C == row).astype(F32)
    return outer, inner


def mode_products(arrived, weights, spectrum, grad_hat):
    total = add_up(arrived).astype(BF16)
    spectrum[...] = total
    modes = total.shape[1] // 2
    outer, inner = repeat_tables()
    grads = dot(total[C:], inner.astype(BF16), ((0,), (0,)))
    scale = mode_scale(modes, modes // MY)
    real_d = grads[:modes] * scale
    imag_d = grads[modes:] * scale
    real_w = weights[0, 0].astype(F32).reshape(modes, C * C)
    imag_w = weights[1, 0].astype(F32).reshape(modes, C * C)
    products = jnp.concatenate(
        [real_w * real_d + imag_w * imag_d, real_w * imag_d - imag_w * real_d], axis=0
    )
    values = None
    for _ in range(3):
        piece = products.astype(BF16)
        products = products - piece.astype(F32)
        term = dot(outer.astype(BF16), piece, ((1,), (1,)))
        values = term if values is None else values + term
    values = values.astype(BF16)
    grad_hat[...] = jnp.broadcast_to(values[None], grad_hat.shape)


def weight_grads(both, result):
    modes = both.shape[2] // 2
    outer, inner = repeat_tables()
    outer = outer.astype(BF16)
    inner = inner.astype(BF16)
    scale = mode_scale(modes, modes // MY)
    real_sum = jnp.zeros((modes, C * C), F32)
    imag_sum = jnp.zeros((modes, C * C), F32)
    for sample in range(both.shape[0]):
        values = both[sample]
        field = dot(values[:C], outer, ((0,), (0,)))
        grads = dot(values[C:], inner, ((0,), (0,)))
        real_u, imag_u = field[:modes], field[modes:]
        real_d, imag_d = grads[:modes] * scale, grads[modes:] * scale
        real_sum = real_sum + (real_u * real_d + imag_u * imag_d)
        imag_sum = imag_sum + (real_u * imag_d - imag_u * real_d)
    for part, total in enumerate((real_sum, imag_sum)):
        result[part, 0] = total.reshape(result.shape[2:])


def pair_spectra(own, other, both):
    both[0] = own[...]
    both[1] = other[...]


def inverse_x(arrived, x_rows, result):
    blocks = x_blocks(x_rows)
    values = arrived[...].reshape(MX * C, arrived.shape[2])
    half = values.shape[1] // 2
    swapped = jnp.concatenate([-values[:, half:], values[:, :half]], axis=1)
    sums = dot(values, blocks[0], ((0,), (0,))) + dot(swapped, blocks[1], ((0,), (0,)))
    result[...] = jnp.broadcast_to(sums.astype(BF16)[None], result.shape)


def mixing_table(point, rows):
    local_x = rows // C
    row = lax.broadcasted_iota(jnp.int32, (rows, C), 0) // local_x
    pick = (row == lax.broadcasted_iota(jnp.int32, (rows, C), 1)).astype(BF16)
    spread = dot(pick, point[...], ((1,), (0,))).astype(BF16)
    spread = dot(spread, pick, ((1,), (1,)))
    left = lax.broadcasted_iota(jnp.int32, (rows, rows), 0) % local_x
    right = lax.broadcasted_iota(jnp.int32, (rows, rows), 1) % local_x
    return jnp.where(left == right, spread, 0.0).astype(BF16)


def inverse_yz(
    own, taken, grad_pre, z_table, y_tables, point, both, result, grad_spec,
    lines, staged, spec_staged, sems, spec_sem,
):
    y_table = y_tables[lax.axis_index("gy")]
    rows = staged.shape[0]
    mixing = mixing_table(point, rows)
    side = lax.axis_index("gy") % 2
    per = MZ // own.shape[0]
    for index in range(own.shape[0]):
        for spectra, offset in ((own, side), (taken, 1 - side)):
            block = dot(y_table, spectra[index], ((0,), (0,)))
            first = (2 * index + offset) * per
            lines[pl.ds(first, per)] = block.reshape(per, -1, rows)
    weight_grads(both, spec_staged)
    spec_copy = pltpu.make_async_copy(spec_staged, grad_spec, spec_sem)
    spec_copy.start()
    width = z_table.shape[1]
    copies = [spec_copy]
    for group in range(result.shape[1] // width):
        block = lines[:, group * GROUP : (group + 1) * GROUP, :]
        block = block.reshape(2 * MZ * GROUP, rows).astype(BF16)
        part = slice(group * width, (group + 1) * width)
        spectral = dot(block, z_table[...], ((0,), (0,)))
        mixed = dot(mixing, grad_pre[:, part], ((1,), (0,)))
        staged[:, part] = (spectral + mixed).astype(BF16)
        copy = pltpu.make_async_copy(
            staged.at[:, pl.ds(group * width, width)],
            result.at[:, pl.ds(group * width, width)],
            sems.at[group],
        )
        copy.start()
        copies.append(copy)
    for copy in copies:
        copy.wait()


VMEM = pl.BlockSpec(memory_space=pltpu.VMEM)
HBM = pl.BlockSpec(memory_space=pltpu.HBM)


def call(body, ins, outs, scratch=(), vmem=24):
    values = [
        pltpu.with_memory_space_constraint(value, spec.memory_space) for value, spec in ins
    ]
    specs = [spec for _, spec in ins]
    shapes = [
        pltpu.VMEM(shape, dtype) if spec is VMEM else jax.ShapeDtypeStruct(shape, dtype)
        for shape, dtype, spec in outs
    ]
    return pl.pallas_call(
        body,
        in_specs=specs,
        out_specs=[spec for _, _, spec in outs],
        out_shape=shapes,
        scratch_shapes=list(scratch),
        compiler_params=pltpu.CompilerParams(vmem_limit_bytes=vmem << 20),
    )(*values)


def run_forward_zy(fields, pre_act, cotangent, z_table, y_table, local_mz):
    rows, local_yz = fields.shape
    local_y = local_yz // NZ
    modes = MY * local_mz
    half = (MZ // local_mz // 2, 2 * modes, 2 * rows)
    whole = (rows, local_yz)
    dma = pltpu.SemaphoreType.DMA
    return call(
        forward_zy,
        [(fields, HBM), (pre_act, HBM), (cotangent, HBM), (z_table, HBM), (y_table, HBM)],
        [(whole, BF16, VMEM), (half, BF16, VMEM), (half, BF16, VMEM)],
        [pltpu.VMEM(whole, BF16)] * 3
        + [
            pltpu.VMEM(z_table.shape, BF16),
            pltpu.VMEM(y_table.shape[1:], BF16),
            pltpu.VMEM((2 * MZ, local_y, 2 * rows), BF16),
            dma((3, 2)),
            dma((2,)),
        ],
    )


def run_inverse_yz(own, taken, grad_pre, z_table, y_table, point, both, spec_shape):
    rows, local_yz = grad_pre.shape
    local_y = local_yz // NZ
    groups = local_y // GROUP
    return call(
        inverse_yz,
        [
            (own, VMEM),
            (taken, VMEM),
            (grad_pre, VMEM),
            (z_table, VMEM),
            (y_table, VMEM),
            (point, VMEM),
            (both, VMEM),
        ],
        [((rows, local_yz), BF16, HBM), (spec_shape, F32, HBM)],
        [
            pltpu.VMEM((2 * MZ, local_y, rows), F32),
            pltpu.VMEM((rows, local_yz), BF16),
            pltpu.VMEM(spec_shape, F32),
            pltpu.SemaphoreType.DMA((groups,)),
            pltpu.SemaphoreType.DMA(()),
        ],
    )


def exchange(pieces, axis, groups=None):
    return lax.all_to_all(
        pieces, axis, split_axis=0, concat_axis=0, tiled=True, axis_index_groups=groups
    )


def on_device(fields, pre_act, cotangent, spec_weight, point_weight):
    count_x = lax.axis_size("gx")
    count_y = lax.axis_size("gy")
    _, channels, local_x, local_yz = fields.shape
    local_y = local_yz // NZ
    local_mz = spec_weight.shape[3]
    rows = channels * local_x
    modes = MY * local_mz
    z_table = jnp.asarray(z_block_table())
    y_table = jnp.asarray(y_block_tables(count_y, local_y, local_mz))
    x_rows = jnp.asarray(x_row_tables(count_x, local_x))
    whole = (rows, local_yz)

    grad_pre, kept, given = run_forward_zy(
        fields.reshape(whole),
        pre_act.reshape(whole),
        cotangent.reshape(whole),
        z_table,
        y_table,
        local_mz,
    )
    other_side = [(i, i ^ 1) for i in range(count_y)]
    taken = lax.ppermute(given, "gy", other_side)
    (sums,) = call(add_halves, [(kept, VMEM), (taken, VMEM)], [(kept.shape, BF16, VMEM)])
    sides = [list(range(side, count_y, 2)) for side in range(2)]
    arrived = exchange(sums, "gy", sides)
    (pieces,) = call(
        forward_x,
        [(arrived, VMEM), (x_rows, VMEM)],
        [((count_x, 2 * C, 2 * modes), BF16, VMEM)],
    )
    arrived = exchange(pieces, "gx")
    spectrum, pieces = call(
        mode_products,
        [(arrived, VMEM), (spec_weight, VMEM)],
        [((2 * C, 2 * modes), BF16, VMEM), ((count_x, C, 2 * modes), BF16, VMEM)],
    )
    arrived = exchange(pieces, "gx")
    other = lax.ppermute(spectrum, "dp", [(0, 1), (1, 0)])
    (both,) = call(
        pair_spectra,
        [(spectrum, VMEM), (other, VMEM)],
        [((2,) + spectrum.shape, BF16, VMEM)],
    )
    (pieces,) = call(
        inverse_x,
        [(arrived, VMEM), (x_rows, VMEM)],
        [((count_y // 2, 2 * modes, rows), BF16, VMEM)],
    )
    own = exchange(pieces, "gy", sides)
    taken = lax.ppermute(own, "gy", other_side)
    grad_fields, grad_spec = run_inverse_yz(
        own, taken, grad_pre, z_table, y_table, point_weight, both, spec_weight.shape
    )
    return grad_fields.reshape(fields.shape), grad_spec


def solution(mesh):
    placed = (
        P("dp", None, "gx", "gy"),
        P("dp", None, "gx", "gy"),
        P("dp", None, "gx", "gy"),
        P(None, "gx", None, "gy", None),
        P(),
    )

    return jax.shard_map(
        on_device,
        mesh=mesh,
        in_specs=placed,
        out_specs=(P("dp", None, "gx", "gy"), P(None, "gx", None, "gy", None)),
        check_vma=False,
    )
```

profile of v0, /device:TPU:1, one launch (start us, length us, event | category | flops | bytes accessed | tf_op | source)
XLA Modules:
  0.0 85.3 jit_solution(13867449221882236151)
XLA Ops:
  0.6 3.4 %shard_map.95 = (bf16[128,4096]{1,0:T(8,128)(2,1)S(1)}, bf16[4,128,256]{2,1,0:T(8,128)(2,1)S(1)}, bf16[4,128,256]{2,1,0:T(8,128)(2,1)S(1)}) custom-call(bf16[128,4096]{1,0:T(8,128)(2,1)} %bitcast.4, bf16[128,4096]{1,0:T(8,128)(2,1)} %bitcast.5, bf16[128,4096]{1,0:T(8,128)(2,1)} %bitcast.6, bf16[256,512]{1,0:T(8,128)(2,1)} %constant.6.clone.z_source.z_table, ...), custom_call_target="tpu_custom_call" | custom-call | tf_op jit(solution)/shard_map/pallas_call | solution.py:307
  4.1 8.7 %collective-permute-start = (bf16[4,128,256]{2,1,0:T(8,128)(2,1)S(1)}, bf16[4,128,256]{2,1,0:T(8,128)(2,1)S(1)}, u32[]{:S(2)}, u32[]{:S(2)}) collective-permute-start(bf16[4,128,256]{2,1,0:T(8,128)(2,1)S(1)} %get-tuple-element.10), channel_id=1, source_target_pairs={{0,1},{1,0},{2,3},{3,2},{4,5},{5,4},{6,7},{7,6},{8,9},{9,8},{10,11... | collective-permute-start | bytes 786440 | tf_op jit(solution)/shard_map/ppermute | solution.py:393
  12.8 1.1 %collective-permute-done.taken = bf16[4,128,256]{2,1,0:T(8,128)(2,1)S(1)} collective-permute-done((bf16[4,128,256]{2,1,0:T(8,128)(2,1)S(1)}, bf16[4,128,256]{2,1,0:T(8,128)(2,1)S(1)}, u32[]{:S(2)}, u32[]{:S(2)}) %collective-permute-start) | collective-permute-done | bytes 262176 | tf_op jit(solution)/shard_map/ppermute | solution.py:393
  14.0 0.0 copy-start.1
  14.0 0.1 shard_map.96
  14.0 10.8 %all_to_all.20.arrived = bf16[4,128,256]{2,1,0:T(8,128)(2,1)S(1)} all-to-all(bf16[4,128,256]{2,1,0:T(8,128)(2,1)S(1)} %shard_map.96), channel_id=1, replica_groups={{0,2,4,6},{1,3,5,7},{8,10,12,14},{9,11,13,15},{16,18,20,22},{17,19,21,2..., dimensions={0} | all-to-all | bytes 524288 | tf_op jit(solution)/shard_map/all_to_all | solution.py:366
  24.8 0.0 copy-done.1
  24.8 0.3 shard_map.97
  25.1 0.0 copy-start.3
  25.1 18.0 %all_to_all.21.arrived = bf16[32,32,128]{2,1,0:T(8,128)(2,1)S(1)} all-to-all(bf16[32,32,128]{2,1,0:T(8,128)(2,1)S(1)} %shard_map.97), channel_id=1, replica_groups=mesh['dp'=2,'gx'=32,'gy'=8] {'gx'}, dimensions={0} | all-to-all | bytes 524288 | tf_op jit(solution)/shard_map/all_to_all | solution.py:366
  43.1 0.0 copy-done.3
  43.1 0.5 shard_map.98
  43.6 13.6 %all_to_all.22.arrived = bf16[32,16,128]{2,1,0:T(8,128)(2,1)S(1)} all-to-all(bf16[32,16,128]{2,1,0:T(8,128)(2,1)S(1)} %get-tuple-element.11), channel_id=1, replica_groups=mesh['dp'=2,'gx'=32,'gy'=8] {'gx'}, dimensions={0} | all-to-all | bytes 262144 | tf_op jit(solution)/shard_map/all_to_all | solution.py:366
  57.1 0.0 copy-start
  57.1 0.4 shard_map.99
  57.5 0.0 copy-start.2
  57.5 10.3 %all_to_all.23.own = bf16[4,128,128]{2,1,0:T(8,128)(2,1)S(1)} all-to-all(bf16[4,128,128]{2,1,0:T(8,128)(2,1)S(1)} %shard_map.99), channel_id=1, replica_groups={{0,2,4,6},{1,3,5,7},{8,10,12,14},{9,11,13,15},{16,18,20,22},{17,19,21,2..., dimensions={0} | all-to-all | bytes 262144 | tf_op jit(solution)/shard_map/all_to_all | solution.py:366
  67.8 6.6 %collective-permute-start.1 = (bf16[4,128,128]{2,1,0:T(8,128)(2,1)S(1)}, bf16[4,128,128]{2,1,0:T(8,128)(2,1)S(1)}, u32[]{:S(2)}, u32[]{:S(2)}) collective-permute-start(bf16[4,128,128]{2,1,0:T(8,128)(2,1)S(1)} %all_to_all.23.own), channel_id=1, source_target_pairs={{0,1},{1,0},{2,3},{3,2},{4,5},{5,4},{6,7},{7,6},{8,9},{9,8},{10,11... | collective-permute-start | bytes 393224 | tf_op jit(solution)/shard_map/ppermute | solution.py:421
  74.4 5.5 %collective-permute-start.2 = (bf16[32,128]{1,0:T(8,128)(2,1)S(1)}, bf16[32,128]{1,0:T(8,128)(2,1)S(1)}, u32[]{:S(2)}, u32[]{:S(2)}) collective-permute-start(bf16[32,128]{1,0:T(8,128)(2,1)S(1)} %get-tuple-element.13.own), channel_id=1, source_target_pairs={{0,256},{256,0},{1,257},{257,1},{2,258},{258,2},{3,259},{259,3},{4... | collective-permute-start | bytes 24584 | tf_op jit(solution)/shard_map/ppermute | solution.py:409
  79.9 2.8 %collective-permute-done.2.other = bf16[32,128]{1,0:T(8,128)(2,1)S(1)} collective-permute-done((bf16[32,128]{1,0:T(8,128)(2,1)S(1)}, bf16[32,128]{1,0:T(8,128)(2,1)S(1)}, u32[]{:S(2)}, u32[]{:S(2)}) %collective-permute-start.2) | collective-permute-done | bytes 8224 | tf_op jit(solution)/shard_map/ppermute | solution.py:409
  82.7 0.0 copy-start.4
  82.7 0.0 collective-permute-done.1.taken
  82.7 0.0 copy-done
  82.7 0.0 copy-done.2
  82.7 0.7 copy-done.4
  83.4 1.9 %shard_map.101 = (bf16[128,4096]{1,0:T(8,128)(2,1)}, f32[2,1,32,2,256]{4,3,2,1,0:T(2,128)}) custom-call(bf16[4,128,128]{2,1,0:T(8,128)(2,1)S(1)} %all_to_all.23.own, bf16[4,128,128]{2,1,0:T(8,128)(2,1)S(1)} %collective-permute-done.1.taken, bf16[128,4096]{1,0:T(8,128)(2,1)S(1)} %get-tuple-element.12.grad_pre, bf16[256,512]{1,0:T(8,128)(2,1)S(1)} %copy-done.2, ...), custom_call_target="tpu_custom_call" | custom-call | tf_op jit(solution)/shard_map/pallas_call | solution.py:307
  (1 shorter events, 0.0 us)
Async XLA Ops:
  4.1 9.9 %collective-permute-start = (bf16[4,128,256]{2,1,0:T(8,128)(2,1)S(1)}, bf16[4,128,256]{2,1,0:T(8,128)(2,1)S(1)}, u32[]{:S(2)}, u32[]{:S(2)}) collective-permute-start(bf16[4,128,256]{2,1,0:T(8,128)(2,1)S(1)} %get-tuple-element.10), channel_id=1, source_target_pairs={{0,1},{1,0},{2,3},{3,2},{4,5},{5,4},{6,7},{7,6},{8,9},{9,8},{10,11... | collective-permute-start | bytes 786440 | tf_op jit(solution)/shard_map/ppermute | solution.py:393
  14.0 10.8 %copy-start.1 = (bf16[32,2,32,128]{3,2,1,0:T(8,128)(2,1)S(1)}, bf16[32,2,32,128]{3,2,1,0:T(8,128)(2,1)}, u32[]{:S(2)}) copy-start(bf16[32,2,32,128]{3,2,1,0:T(8,128)(2,1)} %constant.8.clone.x_rows) | copy-start | bytes 1572868
  25.1 18.0 %copy-start.3 = (bf16[2,1,32,2,256]{4,3,2,1,0:T(2,128)(2,1)S(1)}, bf16[2,1,32,2,256]{4,3,2,1,0:T(2,128)(2,1)}, u32[]{:S(2)}) copy-start(bf16[2,1,32,2,256]{4,3,2,1,0:T(2,128)(2,1)} %weights.1) | copy-start | bytes 196612
  57.1 25.6 %copy-start = (bf16[8,128,256]{2,1,0:T(8,128)(2,1)S(1)}, bf16[8,128,256]{2,1,0:T(8,128)(2,1)}, u32[]{:S(2)}) copy-start(bf16[8,128,256]{2,1,0:T(8,128)(2,1)} %constant.7.clone.y_source.y_tables) | copy-start | bytes 1572868
  57.5 25.2 %copy-start.2 = (bf16[256,512]{1,0:T(8,128)(2,1)S(1)}, bf16[256,512]{1,0:T(8,128)(2,1)}, u32[]{:S(2)}) copy-start(bf16[256,512]{1,0:T(8,128)(2,1)} %constant.6.clone.z_source.z_table) | copy-start | bytes 786436
  67.8 14.9 %collective-permute-start.1 = (bf16[4,128,128]{2,1,0:T(8,128)(2,1)S(1)}, bf16[4,128,128]{2,1,0:T(8,128)(2,1)S(1)}, u32[]{:S(2)}, u32[]{:S(2)}) collective-permute-start(bf16[4,128,128]{2,1,0:T(8,128)(2,1)S(1)} %all_to_all.23.own), channel_id=1, source_target_pairs={{0,1},{1,0},{2,3},{3,2},{4,5},{5,4},{6,7},{7,6},{8,9},{9,8},{10,11... | collective-permute-start | bytes 393224 | tf_op jit(solution)/shard_map/ppermute | solution.py:421
  74.4 8.3 %collective-permute-start.2 = (bf16[32,128]{1,0:T(8,128)(2,1)S(1)}, bf16[32,128]{1,0:T(8,128)(2,1)S(1)}, u32[]{:S(2)}, u32[]{:S(2)}) collective-permute-start(bf16[32,128]{1,0:T(8,128)(2,1)S(1)} %get-tuple-element.13.own), channel_id=1, source_target_pairs={{0,256},{256,0},{1,257},{257,1},{2,258},{258,2},{3,259},{259,3},{4... | collective-permute-start | bytes 24584 | tf_op jit(solution)/shard_map/ppermute | solution.py:409
  82.7 0.7 copy-start.4
where the time goes:
time: 85.7 us; the launch traced here: 85.3 us
  blocking collectives  52.6 us (61%)
  starting transfers between devices  20.8 us (24%)
  Pallas kernels  6.54 us (8%)
  waiting for transfers between devices  3.93 us (5%)
    all_to_all x4, blocking collectives, exchange(): lax.all_to_all(pieces, axis, split_axis=0, concat_axis=0, tiled=True, axi...  52.6 us
    ppermute x1, starting transfers between devices, on_device(): taken = lax.ppermute(given, 'gy', other_side)  8.75 us
    ppermute x1, starting transfers between devices, on_device(): taken = lax.ppermute(own, 'gy', other_side)  6.55 us
    pallas_call x7, Pallas kernels, call(): pl.pallas_call(body, in_specs=specs, out_specs=[spec for _, _, spec in ou...  6.54 us
    ppermute x1, starting transfers between devices, on_device(): other = lax.ppermute(spectrum, 'dp', [(0, 1), (1, 0)])  5.5 us
    ppermute x1, waiting for transfers between devices, on_device(): other = lax.ppermute(spectrum, 'dp', [(0, 1), (1, 0)])  2.79 us
  transfers between devices with their start and end apart: 3, of which 2 were waited for; matrix products, arithmetic and copies ran while one was open for 0% of the time, Pallas kernels for 0%

commit v1 on v0

--- a/solution.py
+++ b/solution.py
@@ -254,25 +254,31 @@
     return jnp.where(left == right, spread, 0.0).astype(BF16)
 
 
+def inverse_y(own, y_tables, both, own_lines, grad_spec, spec_staged, spec_sem):
+    weight_grads(both, spec_staged)
+    spec_copy = pltpu.make_async_copy(spec_staged, grad_spec, spec_sem)
+    spec_copy.start()
+    y_table = y_tables[lax.axis_index("gy")]
+    for index in range(own.shape[0]):
+        block = dot(y_table, own[index], ((0,), (0,)))
+        own_lines[index] = block.reshape(own_lines.shape[1:])
+    spec_copy.wait()
+
+
 def inverse_yz(
-    own, taken, grad_pre, z_table, y_tables, point, both, result, grad_spec,
-    lines, staged, spec_staged, sems, spec_sem,
+    own_lines, taken, grad_pre, z_table, y_tables, point, result, lines, staged, sems
 ):
     y_table = y_tables[lax.axis_index("gy")]
     rows = staged.shape[0]
     mixing = mixing_table(point, rows)
     side = lax.axis_index("gy") % 2
-    per = MZ // own.shape[0]
-    for index in range(own.shape[0]):
-        for spectra, offset in ((own, side), (taken, 1 - side)):
-            block = dot(y_table, spectra[index], ((0,), (0,)))
-            first = (2 * index + offset) * per
-            lines[pl.ds(first, per)] = block.reshape(per, -1, rows)
-    weight_grads(both, spec_staged)
-    spec_copy = pltpu.make_async_copy(spec_staged, grad_spec, spec_sem)
-    spec_copy.start()
+    per = own_lines.shape[1]
+    for index in range(taken.shape[0]):
+        block = dot(y_table, taken[index], ((0,), (0,)))
+        lines[pl.ds((2 * index + 1 - side) * per, per)] = block.reshape(per, -1, rows)
+        lines[pl.ds((2 * index + side) * per, per)] = own_lines[index]
     width = z_table.shape[1]
-    copies = [spec_copy]
+    copies = []
     for group in range(result.shape[1] // width):
         block = lines[:, group * GROUP : (group + 1) * GROUP, :]
         block = block.reshape(2 * MZ * GROUP, rows).astype(BF16)
@@ -336,30 +342,41 @@
     )
 
 
-def run_inverse_yz(own, taken, grad_pre, z_table, y_table, point, both, spec_shape):
+def run_inverse_y(own, y_table, both, spec_shape):
+    count, _, rows = own.shape
+    return call(
+        inverse_y,
+        [(own, VMEM), (y_table, VMEM), (both, VMEM)],
+        [
+            ((count, MZ // count, y_table.shape[2] * count // MZ, rows), F32, VMEM),
+            (spec_shape, F32, HBM),
+        ],
+        [pltpu.VMEM(spec_shape, F32), pltpu.SemaphoreType.DMA(())],
+    )
+
+
+def run_inverse_yz(own_lines, taken, grad_pre, z_table, y_table, point):
     rows, local_yz = grad_pre.shape
     local_y = local_yz // NZ
     groups = local_y // GROUP
-    return call(
+    (grad_fields,) = call(
         inverse_yz,
         [
-            (own, VMEM),
+            (own_lines, VMEM),
             (taken, VMEM),
             (grad_pre, VMEM),
             (z_table, VMEM),
             (y_table, VMEM),
             (point, VMEM),
-            (both, VMEM),
         ],
-        [((rows, local_yz), BF16, HBM), (spec_shape, F32, HBM)],
+        [((rows, local_yz), BF16, HBM)],
         [
             pltpu.VMEM((2 * MZ, local_y, rows), F32),
             pltpu.VMEM((rows, local_yz), BF16),
-            pltpu.VMEM(spec_shape, F32),
             pltpu.SemaphoreType.DMA((groups,)),
-            pltpu.SemaphoreType.DMA(()),
         ],
     )
+    return grad_fields
 
 
 def exchange(pieces, axis, groups=None):
@@ -419,9 +436,8 @@
     )
     own = exchange(pieces, "gy", sides)
     taken = lax.ppermute(own, "gy", other_side)
-    grad_fields, grad_spec = run_inverse_yz(
-        own, taken, grad_pre, z_table, y_table, point_weight, both, spec_weight.shape
-    )
+    own_lines, grad_spec = run_inverse_y(own, y_table, both, spec_weight.shape)
+    grad_fields = run_inverse_yz(own_lines, taken, grad_pre, z_table, y_table, point_weight)
     return grad_fields.reshape(fields.shape), grad_spec
 
 

time: 85.7 us -> 85.8 us (level)
  Pallas kernels: 6.54 us -> 7.42 us
    pallas_call x7 -> x8, Pallas kernels: 6.54 us -> 7.42 us  [call(): pl.pallas_call(body, in_specs=specs, out_specs=[spec for _, _, spec in ou...]
  transfers between devices with their start and end apart: 3 -> 3, of which waited for: 2 -> 2; matrix products, arithmetic and copies ran while one was open for 0% -> 0% of each run, Pallas kernels for 0% -> 1%
where the time goes in v1:
time: 85.8 us; the launch traced here: 85.4 us
  blocking collectives  52.5 us (61%)
  starting transfers between devices  20.8 us (24%)
  Pallas kernels  7.42 us (9%)
  waiting for transfers between devices  3.93 us (5%)
    all_to_all x4, blocking collectives, exchange(): lax.all_to_all(pieces, axis, split_axis=0, concat_axis=0, tiled=True, axi...  52.5 us
    ppermute x1, starting transfers between devices, on_device(): taken = lax.ppermute(given, 'gy', other_side)  8.75 us
    pallas_call x8, Pallas kernels, call(): pl.pallas_call(body, in_specs=specs, out_specs=[spec for _, _, spec in ou...  7.42 us
    ppermute x1, starting transfers between devices, on_device(): taken = lax.ppermute(own, 'gy', other_side)  6.55 us
    ppermute x1, starting transfers between devices, on_device(): other = lax.ppermute(spectrum, 'dp', [(0, 1), (1, 0)])  5.5 us
    ppermute x1, waiting for transfers between devices, on_device(): other = lax.ppermute(spectrum, 'dp', [(0, 1), (1, 0)])  2.79 us
  transfers between devices with their start and end apart: 3, of which 2 were waited for; matrix products, arithmetic and copies ran while one was open for 0% of the time, Pallas kernels for 1%

profile of v1, /device:TPU:1, one launch (start us, length us, event | category | flops | bytes accessed | tf_op | source)
XLA Modules:
  0.0 85.4 jit_solution(5019014885913256855)
XLA Ops:
  0.6 3.4 %shard_map.95 = (bf16[128,4096]{1,0:T(8,128)(2,1)S(1)}, bf16[4,128,256]{2,1,0:T(8,128)(2,1)S(1)}, bf16[4,128,256]{2,1,0:T(8,128)(2,1)S(1)}) custom-call(bf16[128,4096]{1,0:T(8,128)(2,1)} %bitcast.4, bf16[128,4096]{1,0:T(8,128)(2,1)} %bitcast.5, bf16[128,4096]{1,0:T(8,128)(2,1)} %bitcast.6, bf16[256,512]{1,0:T(8,128)(2,1)} %constant.6.clone.z_source.z_table, ...), custom_call_target="tpu_custom_call" | custom-call | tf_op jit(solution)/shard_map/pallas_call | solution.py:313
  4.1 8.7 %collective-permute-start = (bf16[4,128,256]{2,1,0:T(8,128)(2,1)S(1)}, bf16[4,128,256]{2,1,0:T(8,128)(2,1)S(1)}, u32[]{:S(2)}, u32[]{:S(2)}) collective-permute-start(bf16[4,128,256]{2,1,0:T(8,128)(2,1)S(1)} %get-tuple-element.10), channel_id=1, source_target_pairs={{0,1},{1,0},{2,3},{3,2},{4,5},{5,4},{6,7},{7,6},{8,9},{9,8},{10,11... | collective-permute-start | bytes 786440 | tf_op jit(solution)/shard_map/ppermute | solution.py:410
  12.8 1.1 %collective-permute-done.taken = bf16[4,128,256]{2,1,0:T(8,128)(2,1)S(1)} collective-permute-done((bf16[4,128,256]{2,1,0:T(8,128)(2,1)S(1)}, bf16[4,128,256]{2,1,0:T(8,128)(2,1)S(1)}, u32[]{:S(2)}, u32[]{:S(2)}) %collective-permute-start) | collective-permute-done | bytes 262176 | tf_op jit(solution)/shard_map/ppermute | solution.py:410
  14.0 0.0 copy-start.1
  14.0 0.1 shard_map.96
  14.0 10.8 %all_to_all.20.arrived = bf16[4,128,256]{2,1,0:T(8,128)(2,1)S(1)} all-to-all(bf16[4,128,256]{2,1,0:T(8,128)(2,1)S(1)} %shard_map.96), channel_id=1, replica_groups={{0,2,4,6},{1,3,5,7},{8,10,12,14},{9,11,13,15},{16,18,20,22},{17,19,21,2..., dimensions={0} | all-to-all | bytes 524288 | tf_op jit(solution)/shard_map/all_to_all | solution.py:383
  24.8 0.0 copy-done.1
  24.8 0.3 shard_map.97
  25.1 0.0 copy-start.3
  25.1 18.0 %all_to_all.21.arrived = bf16[32,32,128]{2,1,0:T(8,128)(2,1)S(1)} all-to-all(bf16[32,32,128]{2,1,0:T(8,128)(2,1)S(1)} %shard_map.97), channel_id=1, replica_groups=mesh['dp'=2,'gx'=32,'gy'=8] {'gx'}, dimensions={0} | all-to-all | bytes 524288 | tf_op jit(solution)/shard_map/all_to_all | solution.py:383
  43.1 0.0 copy-done.3
  43.1 0.5 shard_map.98
  43.6 13.6 %all_to_all.22.arrived = bf16[32,16,128]{2,1,0:T(8,128)(2,1)S(1)} all-to-all(bf16[32,16,128]{2,1,0:T(8,128)(2,1)S(1)} %get-tuple-element.11), channel_id=1, replica_groups=mesh['dp'=2,'gx'=32,'gy'=8] {'gx'}, dimensions={0} | all-to-all | bytes 262144 | tf_op jit(solution)/shard_map/all_to_all | solution.py:383
  57.1 0.0 copy-start
  57.1 0.4 shard_map.99
  57.5 10.2 %all_to_all.23.own = bf16[4,128,128]{2,1,0:T(8,128)(2,1)S(1)} all-to-all(bf16[4,128,128]{2,1,0:T(8,128)(2,1)S(1)} %shard_map.99), channel_id=1, replica_groups={{0,2,4,6},{1,3,5,7},{8,10,12,14},{9,11,13,15},{16,18,20,22},{17,19,21,2..., dimensions={0} | all-to-all | bytes 262144 | tf_op jit(solution)/shard_map/all_to_all | solution.py:383
  67.7 6.6 %collective-permute-start.2 = (bf16[4,128,128]{2,1,0:T(8,128)(2,1)S(1)}, bf16[4,128,128]{2,1,0:T(8,128)(2,1)S(1)}, u32[]{:S(2)}, u32[]{:S(2)}) collective-permute-start(bf16[4,128,128]{2,1,0:T(8,128)(2,1)S(1)} %all_to_all.23.own), channel_id=1, source_target_pairs={{0,1},{1,0},{2,3},{3,2},{4,5},{5,4},{6,7},{7,6},{8,9},{9,8},{10,11... | collective-permute-start | bytes 393224 | tf_op jit(solution)/shard_map/ppermute | solution.py:438
  74.3 5.5 %collective-permute-start.1 = (bf16[32,128]{1,0:T(8,128)(2,1)S(1)}, bf16[32,128]{1,0:T(8,128)(2,1)S(1)}, u32[]{:S(2)}, u32[]{:S(2)}) collective-permute-start(bf16[32,128]{1,0:T(8,128)(2,1)S(1)} %get-tuple-element.12.own), channel_id=1, source_target_pairs={{0,256},{256,0},{1,257},{257,1},{2,258},{258,2},{3,259},{259,3},{4... | collective-permute-start | bytes 24584 | tf_op jit(solution)/shard_map/ppermute | solution.py:426
  79.8 2.8 %collective-permute-done.1.other = bf16[32,128]{1,0:T(8,128)(2,1)S(1)} collective-permute-done((bf16[32,128]{1,0:T(8,128)(2,1)S(1)}, bf16[32,128]{1,0:T(8,128)(2,1)S(1)}, u32[]{:S(2)}, u32[]{:S(2)}) %collective-permute-start.1) | collective-permute-done | bytes 8224 | tf_op jit(solution)/shard_map/ppermute | solution.py:426
  82.6 0.0 copy-done
  82.6 0.0 copy-start.2
  82.6 0.0 copy-start.4
  82.6 1.0 %shard_map.101 = (f32[4,4,64,128]{3,2,1,0:T(8,128)S(1)}, f32[2,1,32,2,256]{4,3,2,1,0:T(2,128)}) custom-call(bf16[4,128,128]{2,1,0:T(8,128)(2,1)S(1)} %all_to_all.23.own, bf16[8,128,256]{2,1,0:T(8,128)(2,1)S(1)} %copy-done, bf16[2,32,128]{2,1,0:T(8,128)(2,1)S(1)} %shard_map.100.both), custom_call_target="tpu_custom_call" | custom-call | tf_op jit(solution)/shard_map/pallas_call | solution.py:313
  83.5 0.0 collective-permute-done.2.taken
  83.6 0.0 copy-done.2
  83.6 0.0 copy-done.4
  83.6 1.8 %shard_map.102 = bf16[128,4096]{1,0:T(8,128)(2,1)} custom-call(f32[4,4,64,128]{3,2,1,0:T(8,128)S(1)} %get-tuple-element.13.own_lines, bf16[4,128,128]{2,1,0:T(8,128)(2,1)S(1)} %collective-permute-done.2.taken, bf16[128,4096]{1,0:T(8,128)(2,1)S(1)} %get-tuple-element.14.grad_pre, bf16[256,512]{1,0:T(8,128)(2,1)S(1)} %copy-done.2, ...), custom_call_target="tpu_custom_call" | custom-call | tf_op jit(solution)/shard_map/pallas_call | solution.py:313
  (1 shorter events, 0.0 us)
Async XLA Ops:
  4.1 9.9 %collective-permute-start = (bf16[4,128,256]{2,1,0:T(8,128)(2,1)S(1)}, bf16[4,128,256]{2,1,0:T(8,128)(2,1)S(1)}, u32[]{:S(2)}, u32[]{:S(2)}) collective-permute-start(bf16[4,128,256]{2,1,0:T(8,128)(2,1)S(1)} %get-tuple-element.10), channel_id=1, source_target_pairs={{0,1},{1,0},{2,3},{3,2},{4,5},{5,4},{6,7},{7,6},{8,9},{9,8},{10,11... | collective-permute-start | bytes 786440 | tf_op jit(solution)/shard_map/ppermute | solution.py:410
  14.0 10.8 %copy-start.1 = (bf16[32,2,32,128]{3,2,1,0:T(8,128)(2,1)S(1)}, bf16[32,2,32,128]{3,2,1,0:T(8,128)(2,1)}, u32[]{:S(2)}) copy-start(bf16[32,2,32,128]{3,2,1,0:T(8,128)(2,1)} %constant.8.clone.x_rows) | copy-start | bytes 1572868
  25.1 18.0 %copy-start.3 = (bf16[2,1,32,2,256]{4,3,2,1,0:T(2,128)(2,1)S(1)}, bf16[2,1,32,2,256]{4,3,2,1,0:T(2,128)(2,1)}, u32[]{:S(2)}) copy-start(bf16[2,1,32,2,256]{4,3,2,1,0:T(2,128)(2,1)} %weights.1) | copy-start | bytes 196612
  57.1 25.4 %copy-start = (bf16[8,128,256]{2,1,0:T(8,128)(2,1)S(1)}, bf16[8,128,256]{2,1,0:T(8,128)(2,1)}, u32[]{:S(2)}) copy-start(bf16[8,128,256]{2,1,0:T(8,128)(2,1)} %constant.7.clone.y_source.y_tables) | copy-start | bytes 1572868
  67.7 15.8 %collective-permute-start.2 = (bf16[4,128,128]{2,1,0:T(8,128)(2,1)S(1)}, bf16[4,128,128]{2,1,0:T(8,128)(2,1)S(1)}, u32[]{:S(2)}, u32[]{:S(2)}) collective-permute-start(bf16[4,128,128]{2,1,0:T(8,128)(2,1)S(1)} %all_to_all.23.own), channel_id=1, source_target_pairs={{0,1},{1,0},{2,3},{3,2},{4,5},{5,4},{6,7},{7,6},{8,9},{9,8},{10,11... | collective-permute-start | bytes 393224 | tf_op jit(solution)/shard_map/ppermute | solution.py:438
  74.3 8.3 %collective-permute-start.1 = (bf16[32,128]{1,0:T(8,128)(2,1)S(1)}, bf16[32,128]{1,0:T(8,128)(2,1)S(1)}, u32[]{:S(2)}, u32[]{:S(2)}) collective-permute-start(bf16[32,128]{1,0:T(8,128)(2,1)S(1)} %get-tuple-element.12.own), channel_id=1, source_target_pairs={{0,256},{256,0},{1,257},{257,1},{2,258},{258,2},{3,259},{259,3},{4... | collective-permute-start | bytes 24584 | tf_op jit(solution)/shard_map/ppermute | solution.py:426
  82.6 1.0 %copy-start.2 = (bf16[256,512]{1,0:T(8,128)(2,1)S(1)}, bf16[256,512]{1,0:T(8,128)(2,1)}, u32[]{:S(2)}) copy-start(bf16[256,512]{1,0:T(8,128)(2,1)} %constant.6.clone.z_source.z_table) | copy-start | bytes 786436
  82.6 1.0 %copy-start.4 = (bf16[16,16]{1,0:T(8,128)(2,1)S(1)}, bf16[16,16]{1,0:T(8,128)(2,1)}, u32[]{:S(2)}) copy-start(bf16[16,16]{1,0:T(8,128)(2,1)} %point.1) | copy-start | bytes 1540

commit v2 on v0

--- a/solution.py
+++ b/solution.py
@@ -255,19 +255,17 @@
 
 
 def inverse_yz(
-    own, taken, grad_pre, z_table, y_tables, point, both, result, grad_spec,
+    arrived, grad_pre, z_table, y_tables, point, both, result, grad_spec,
     lines, staged, spec_staged, sems, spec_sem,
 ):
     y_table = y_tables[lax.axis_index("gy")]
     rows = staged.shape[0]
     mixing = mixing_table(point, rows)
-    side = lax.axis_index("gy") % 2
-    per = MZ // own.shape[0]
-    for index in range(own.shape[0]):
-        for spectra, offset in ((own, side), (taken, 1 - side)):
-            block = dot(y_table, spectra[index], ((0,), (0,)))
-            first = (2 * index + offset) * per
-            lines[pl.ds(first, per)] = block.reshape(per, -1, rows)
+    count = arrived.shape[0]
+    per = 2 * MZ // count
+    for index in range(count):
+        block = dot(y_table, arrived[index], ((0,), (0,)))
+        lines[index * per : (index + 1) * per] = block.reshape(per, -1, rows)
     weight_grads(both, spec_staged)
     spec_copy = pltpu.make_async_copy(spec_staged, grad_spec, spec_sem)
     spec_copy.start()
@@ -336,15 +334,14 @@
     )
 
 
-def run_inverse_yz(own, taken, grad_pre, z_table, y_table, point, both, spec_shape):
+def run_inverse_yz(arrived, grad_pre, z_table, y_table, point, both, spec_shape):
     rows, local_yz = grad_pre.shape
     local_y = local_yz // NZ
     groups = local_y // GROUP
     return call(
         inverse_yz,
         [
-            (own, VMEM),
-            (taken, VMEM),
+            (arrived, VMEM),
             (grad_pre, VMEM),
             (z_table, VMEM),
             (y_table, VMEM),
@@ -389,8 +386,7 @@
         y_table,
         local_mz,
     )
-    other_side = [(i, i ^ 1) for i in range(count_y)]
-    taken = lax.ppermute(given, "gy", other_side)
+    taken = lax.ppermute(given, "gy", [(i, i ^ 1) for i in range(count_y)])
     (sums,) = call(add_halves, [(kept, VMEM), (taken, VMEM)], [(kept.shape, BF16, VMEM)])
     sides = [list(range(side, count_y, 2)) for side in range(2)]
     arrived = exchange(sums, "gy", sides)
@@ -415,12 +411,11 @@
     (pieces,) = call(
         inverse_x,
         [(arrived, VMEM), (x_rows, VMEM)],
-        [((count_y // 2, 2 * modes, rows), BF16, VMEM)],
-    )
-    own = exchange(pieces, "gy", sides)
-    taken = lax.ppermute(own, "gy", other_side)
+        [((count_y, 2 * modes, rows), BF16, VMEM)],
+    )
+    arrived = exchange(pieces, "gy")
     grad_fields, grad_spec = run_inverse_yz(
-        own, taken, grad_pre, z_table, y_table, point_weight, both, spec_weight.shape
+        arrived, grad_pre, z_table, y_table, point_weight, both, spec_weight.shape
     )
     return grad_fields.reshape(fields.shape), grad_spec
 

time: 85.7 us -> 79.5 us (0.928)
  blocking collectives: 52.6 us -> 42.3 us
  starting transfers between devices: 20.8 us -> 23.6 us
    all_to_all x4 -> x3, blocking collectives: 52.6 us -> 42.3 us  [exchange(): lax.all_to_all(pieces, axis, split_axis=0, concat_axis=0, tiled=True, axi...]
    all_to_all x0 -> x1, starting transfers between devices: none -> 9.24 us  [exchange(): lax.all_to_all(pieces, axis, split_axis=0, concat_axis=0, tiled=True, axi...]
    ppermute x2 -> x1, starting transfers between devices: 15.3 us -> 8.75 us  [on_device(): taken = lax.ppermute(given, 'gy', [(i, i ^ 1) for i in range(count_y)])]
where the time goes in v2:
time: 79.5 us; the launch traced here: 79.1 us
  blocking collectives  42.3 us (53%)
  starting transfers between devices  23.6 us (30%)
  Pallas kernels  7.17 us (9%)
  waiting for transfers between devices  4.65 us (6%)
    all_to_all x3, blocking collectives, exchange(): lax.all_to_all(pieces, axis, split_axis=0, concat_axis=0, tiled=True, axi...  42.3 us
    all_to_all x1, starting transfers between devices, exchange(): lax.all_to_all(pieces, axis, split_axis=0, concat_axis=0, tiled=True, axi...  9.24 us
    ppermute x1, starting transfers between devices, on_device(): taken = lax.ppermute(given, 'gy', [(i, i ^ 1) for i in range(count_y)])  8.75 us
    pallas_call x7, Pallas kernels, call(): pl.pallas_call(body, in_specs=specs, out_specs=[spec for _, _, spec in ou...  7.17 us
    ppermute x1, starting transfers between devices, on_device(): other = lax.ppermute(spectrum, 'dp', [(0, 1), (1, 0)])  5.58 us
    ppermute x1, waiting for transfers between devices, on_device(): other = lax.ppermute(spectrum, 'dp', [(0, 1), (1, 0)])  3.5 us
  transfers between devices with their start and end apart: 3, of which 2 were waited for; matrix products, arithmetic and copies ran while one was open for 0% of the time, Pallas kernels for 0%

profile of v2, /device:TPU:1, one launch (start us, length us, event | category | flops | bytes accessed | tf_op | source)
XLA Modules:
  0.0 79.1 jit_solution(5728657846594078048)
XLA Ops:
  0.6 3.4 %shard_map.95 = (bf16[128,4096]{1,0:T(8,128)(2,1)S(1)}, bf16[4,128,256]{2,1,0:T(8,128)(2,1)S(1)}, bf16[4,128,256]{2,1,0:T(8,128)(2,1)S(1)}) custom-call(bf16[128,4096]{1,0:T(8,128)(2,1)} %bitcast.4, bf16[128,4096]{1,0:T(8,128)(2,1)} %bitcast.5, bf16[128,4096]{1,0:T(8,128)(2,1)} %bitcast.6, bf16[256,512]{1,0:T(8,128)(2,1)} %constant.6.clone.z_source.z_table, ...), custom_call_target="tpu_custom_call" | custom-call | tf_op jit(solution)/shard_map/pallas_call | solution.py:305
  4.1 8.7 %collective-permute-start = (bf16[4,128,256]{2,1,0:T(8,128)(2,1)S(1)}, bf16[4,128,256]{2,1,0:T(8,128)(2,1)S(1)}, u32[]{:S(2)}, u32[]{:S(2)}) collective-permute-start(bf16[4,128,256]{2,1,0:T(8,128)(2,1)S(1)} %get-tuple-element.10), channel_id=1, source_target_pairs={{0,1},{1,0},{2,3},{3,2},{4,5},{5,4},{6,7},{7,6},{8,9},{9,8},{10,11... | collective-permute-start | bytes 786440 | tf_op jit(solution)/shard_map/ppermute | solution.py:389
  12.8 1.1 %collective-permute-done.taken = bf16[4,128,256]{2,1,0:T(8,128)(2,1)S(1)} collective-permute-done((bf16[4,128,256]{2,1,0:T(8,128)(2,1)S(1)}, bf16[4,128,256]{2,1,0:T(8,128)(2,1)S(1)}, u32[]{:S(2)}, u32[]{:S(2)}) %collective-permute-start) | collective-permute-done | bytes 262176 | tf_op jit(solution)/shard_map/ppermute | solution.py:389
  14.0 0.0 copy-start
  14.0 0.1 shard_map.96
  14.0 10.8 %all_to_all.20.arrived = bf16[4,128,256]{2,1,0:T(8,128)(2,1)S(1)} all-to-all(bf16[4,128,256]{2,1,0:T(8,128)(2,1)S(1)} %shard_map.96), channel_id=1, replica_groups={{0,2,4,6},{1,3,5,7},{8,10,12,14},{9,11,13,15},{16,18,20,22},{17,19,21,2..., dimensions={0} | all-to-all | bytes 524288 | tf_op jit(solution)/shard_map/all_to_all | solution.py:363
  24.8 0.0 copy-done
  24.8 0.3 shard_map.97
  25.1 0.0 copy-start.3
  25.1 18.0 %all_to_all.21.arrived = bf16[32,32,128]{2,1,0:T(8,128)(2,1)S(1)} all-to-all(bf16[32,32,128]{2,1,0:T(8,128)(2,1)S(1)} %shard_map.97), channel_id=1, replica_groups=mesh['dp'=2,'gx'=32,'gy'=8] {'gx'}, dimensions={0} | all-to-all | bytes 524288 | tf_op jit(solution)/shard_map/all_to_all | solution.py:363
  43.1 0.0 copy-done.3
  43.1 0.5 shard_map.98
  43.6 13.6 %all_to_all.22.arrived = bf16[32,16,128]{2,1,0:T(8,128)(2,1)S(1)} all-to-all(bf16[32,16,128]{2,1,0:T(8,128)(2,1)S(1)} %get-tuple-element.11), channel_id=1, replica_groups=mesh['dp'=2,'gx'=32,'gy'=8] {'gx'}, dimensions={0} | all-to-all | bytes 262144 | tf_op jit(solution)/shard_map/all_to_all | solution.py:363
  57.1 0.0 copy-start.1
  57.1 1.1 %shard_map.99 = bf16[8,128,128]{2,1,0:T(8,128)(2,1)} custom-call(bf16[32,16,128]{2,1,0:T(8,128)(2,1)S(1)} %all_to_all.22.arrived, bf16[32,2,32,128]{3,2,1,0:T(8,128)(2,1)S(1)} %copy-done), custom_call_target="tpu_custom_call" | custom-call | tf_op jit(solution)/shard_map/pallas_call | solution.py:305
  58.2 0.0 copy-start.2
  58.2 9.2 %all-to-all-start.3 = ((bf16[8,128,128]{2,1,0:T(8,128)(2,1)}), bf16[8,128,128]{2,1,0:T(8,128)(2,1)S(1)}, u32[]{:S(2)}, u32[]{:S(2)}) async-start(bf16[8,128,128]{2,1,0:T(8,128)(2,1)} %shard_map.99), calls=%async_computation.3 | async-start | bytes 524288 | tf_op jit(solution)/shard_map/all_to_all | solution.py:363
  67.5 5.6 %collective-permute-start.1 = (bf16[32,128]{1,0:T(8,128)(2,1)S(1)}, bf16[32,128]{1,0:T(8,128)(2,1)S(1)}, u32[]{:S(2)}, u32[]{:S(2)}) collective-permute-start(bf16[32,128]{1,0:T(8,128)(2,1)S(1)} %get-tuple-element.13.own), channel_id=1, source_target_pairs={{0,256},{256,0},{1,257},{257,1},{2,258},{258,2},{3,259},{259,3},{4... | collective-permute-start | bytes 24584 | tf_op jit(solution)/shard_map/ppermute | solution.py:405
  73.1 3.5 %collective-permute-done.1.other = bf16[32,128]{1,0:T(8,128)(2,1)S(1)} collective-permute-done((bf16[32,128]{1,0:T(8,128)(2,1)S(1)}, bf16[32,128]{1,0:T(8,128)(2,1)S(1)}, u32[]{:S(2)}, u32[]{:S(2)}) %collective-permute-start.1) | collective-permute-done | bytes 8224 | tf_op jit(solution)/shard_map/ppermute | solution.py:405
  76.6 0.0 copy-start.4
  76.6 0.0 all-to-all-done.3.arrived
  76.6 0.0 copy-done.1
  76.6 0.0 copy-done.2
  76.6 0.7 copy-done.4
  77.3 1.8 %shard_map.101 = (bf16[128,4096]{1,0:T(8,128)(2,1)}, f32[2,1,32,2,256]{4,3,2,1,0:T(2,128)}) custom-call(bf16[8,128,128]{2,1,0:T(8,128)(2,1)S(1)} %all-to-all-done.3.arrived, bf16[128,4096]{1,0:T(8,128)(2,1)S(1)} %get-tuple-element.12.grad_pre, bf16[256,512]{1,0:T(8,128)(2,1)S(1)} %copy-done.2, bf16[8,128,256]{2,1,0:T(8,128)(2,1)S(1)} %copy-done.1, ...), custom_call_target="tpu_custom_call" | custom-call | tf_op jit(solution)/shard_map/pallas_call | solution.py:305
  (1 shorter events, 0.0 us)
Async XLA Ops:
  4.1 9.9 %collective-permute-start = (bf16[4,128,256]{2,1,0:T(8,128)(2,1)S(1)}, bf16[4,128,256]{2,1,0:T(8,128)(2,1)S(1)}, u32[]{:S(2)}, u32[]{:S(2)}) collective-permute-start(bf16[4,128,256]{2,1,0:T(8,128)(2,1)S(1)} %get-tuple-element.10), channel_id=1, source_target_pairs={{0,1},{1,0},{2,3},{3,2},{4,5},{5,4},{6,7},{7,6},{8,9},{9,8},{10,11... | collective-permute-start | bytes 786440 | tf_op jit(solution)/shard_map/ppermute | solution.py:389
  14.0 10.8 %copy-start = (bf16[32,2,32,128]{3,2,1,0:T(8,128)(2,1)S(1)}, bf16[32,2,32,128]{3,2,1,0:T(8,128)(2,1)}, u32[]{:S(2)}) copy-start(bf16[32,2,32,128]{3,2,1,0:T(8,128)(2,1)} %constant.8.clone.x_rows) | copy-start | bytes 1572868
  25.1 18.0 %copy-start.3 = (bf16[2,1,32,2,256]{4,3,2,1,0:T(2,128)(2,1)S(1)}, bf16[2,1,32,2,256]{4,3,2,1,0:T(2,128)(2,1)}, u32[]{:S(2)}) copy-start(bf16[2,1,32,2,256]{4,3,2,1,0:T(2,128)(2,1)} %weights.1) | copy-start | bytes 196612
  57.1 19.4 %copy-start.1 = (bf16[8,128,256]{2,1,0:T(8,128)(2,1)S(1)}, bf16[8,128,256]{2,1,0:T(8,128)(2,1)}, u32[]{:S(2)}) copy-start(bf16[8,128,256]{2,1,0:T(8,128)(2,1)} %constant.7.clone.y_source.y_tables) | copy-start | bytes 1572868
  58.2 18.4 %copy-start.2 = (bf16[256,512]{1,0:T(8,128)(2,1)S(1)}, bf16[256,512]{1,0:T(8,128)(2,1)}, u32[]{:S(2)}) copy-start(bf16[256,512]{1,0:T(8,128)(2,1)} %constant.6.clone.z_source.z_table) | copy-start | bytes 786436
  58.2 18.3 %all-to-all-start.3 = ((bf16[8,128,128]{2,1,0:T(8,128)(2,1)}), bf16[8,128,128]{2,1,0:T(8,128)(2,1)S(1)}, u32[]{:S(2)}, u32[]{:S(2)}) async-start(bf16[8,128,128]{2,1,0:T(8,128)(2,1)} %shard_map.99), calls=%async_computation.3 | async-start | bytes 524288 | tf_op jit(solution)/shard_map/all_to_all | solution.py:363
  67.5 9.1 %collective-permute-start.1 = (bf16[32,128]{1,0:T(8,128)(2,1)S(1)}, bf16[32,128]{1,0:T(8,128)(2,1)S(1)}, u32[]{:S(2)}, u32[]{:S(2)}) collective-permute-start(bf16[32,128]{1,0:T(8,128)(2,1)S(1)} %get-tuple-element.13.own), channel_id=1, source_target_pairs={{0,256},{256,0},{1,257},{257,1},{2,258},{258,2},{3,259},{259,3},{4... | collective-permute-start | bytes 24584 | tf_op jit(solution)/shard_map/ppermute | solution.py:405
  76.6 0.7 copy-start.4
